TPU v7x, 32 devices: a whole 2x2x4 slice. The times are simulated.
32 devices in a mesh: dp: 16 (over z, y, x), grp: 2 (over core).
Axes of the slice: x: 2, y: 2, z: 4, core: 2. Of those that a mesh axis runs over, the one named last changes fastest.
Arguments:
- embeds: bfloat16 [8192, 1024], P(('dp', 'grp')), may hold values from -7 to 7
- quality: float32 [8192], P(('dp', 'grp')), may hold values from 0.5 to 2
- domain_ids: int32 [8192], P(('dp', 'grp')), may hold values from 0 to 15, as said below
- domain_weight: float32 [16], replicated, may hold values from 0.5 to 2
- dest: int32 [8192], P(('dp', 'grp')), may hold values from 0 to 31, as said below
- counts: int32 [32], P(('dp', 'grp')), may hold values from 192 to 256, as said below
- winners: int32 [4], replicated, may hold values from 0 to 8191, as said below
Outputs:
- relaid: bfloat16 [16384, 1024], P(('dp', 'grp'))
- residual_gain: float32 [16384], P(('dp', 'grp'))
- chol_rows: float32 [4, 16384], P(None, ('dp', 'grp'))
Inputs may be any that keep to these rules, and one draw needn't show every extreme that they name: Rows 0 to counts - 1 of a device are valid, and one device has 256 valid rows. `dest`: destination device over dp and grp (index over dp+grp); among the valid rows of one device at most 16 name any one destination, and on every device some destination is named by exactly 16 valid rows. `domain_ids`: non-decreasing within each device's rows; a device's rows carry one domain number or two consecutive ones. `winners`: distinct valid rows, on distinct devices.
All inputs are finite; a program needn't handle non-finite values.
Results may differ from a plain program's by a relative error of at most 0.0048.
The roundings to bfloat16 on the way count: a program that leaves them out, or rounds other values in their place, can miss the bound.
Values may be sent and summed in bfloat16 or wider, within the bound.
A program may use at most 64 MiB of HBM per device.

v0:
```python
import jax
import jax.numpy as jnp
from jax import lax
from jax.sharding import PartitionSpec as P

RIDGE = 0.1


def body(embeds, quality, domain_ids, domain_weight, dest, counts, winners):
    shards = lax.axis_size(("dp", "grp"))
    pair_size = lax.axis_size("grp")
    spread_size = lax.axis_size("dp")
    slot_count = embeds.shape[0]
    feature_width = embeds.shape[1]
    step_count = winners.shape[0]
    domains = domain_weight.shape[0]
    per_pair = 2 * slot_count // shards
    balanced = shards * per_pair
    source = lax.axis_index(("dp", "grp"))
    row_index = jnp.arange(slot_count, dtype=jnp.int32)
    is_valid = row_index < counts[0]
    matches = domain_ids[:, None] == jnp.arange(domains, dtype=jnp.int32)[None, :]
    weight_row = jnp.sum(jnp.where(matches, domain_weight[None, :], 0.0), axis=1)
    row_quality = jnp.where(is_valid, quality * weight_row, 0.0).astype(jnp.bfloat16)
    targets = jnp.arange(shards, dtype=jnp.int32)
    dest_hot = ((dest[:, None] == targets[None, :]) & is_valid[:, None]).astype(jnp.bfloat16)
    strictly_lower = (row_index[None, :] < row_index[:, None]).astype(jnp.bfloat16)
    earlier_count = jnp.dot(strictly_lower, dest_hot, preferred_element_type=jnp.float32)
    dest_rank = jnp.sum(jnp.where(dest_hot > 0, earlier_count, 0.0), axis=1).astype(jnp.int32)
    send_slot = jnp.where(is_valid, dest * per_pair + dest_rank, balanced)
    bal_place = (dest * balanced + source * per_pair + dest_rank).astype(jnp.float32)
    send_rows = (
        jnp.zeros((balanced, feature_width), jnp.bfloat16).at[send_slot].set(embeds, mode="drop")
    )
    send_rows = send_rows.reshape(spread_size, pair_size, per_pair, feature_width)
    send_quality = jnp.zeros((balanced,), jnp.bfloat16).at[send_slot].set(row_quality, mode="drop")
    send_quality = send_quality.reshape(spread_size, pair_size, per_pair)
    quality_wide = row_quality.astype(jnp.float32)
    first_hop = (
        lax.all_to_all(send_rows, "dp", split_axis=0, concat_axis=0, tiled=True),
        lax.all_to_all(send_quality, "dp", split_axis=0, concat_axis=0, tiled=True),
    )
    rows_in = lax.all_to_all(first_hop[0], "grp", split_axis=1, concat_axis=1, tiled=True)
    quality_in = lax.all_to_all(first_hop[1], "grp", split_axis=1, concat_axis=1, tiled=True)
    row_norms = jnp.einsum("abmd,abmd->abm", rows_in, rows_in, preferred_element_type=jnp.float32)
    relaid = rows_in.reshape(balanced, feature_width)
    bal_quality = quality_in.reshape(balanced).astype(jnp.float32)
    row_norms = row_norms.reshape(balanced)
    residual_gain = jnp.where(
        bal_quality > 0, bal_quality * bal_quality * row_norms / feature_width + RIDGE, 0.0
    )
    local_place = (source * balanced + jnp.arange(balanced, dtype=jnp.int32)).astype(jnp.float32)
    kept_rows = []
    kept_quality = []
    kept_columns = []
    kept_roots = []
    chol_list = []
    for turn_index in range(step_count):
        chosen = (
            row_index[None, :]
            == (winners[turn_index : turn_index + 1] - source * slot_count)[:, None]
        )
        picked_rows = jnp.dot(
            chosen.astype(jnp.bfloat16), embeds, preferred_element_type=jnp.float32
        )
        picked_quality = jnp.sum(jnp.where(chosen, quality_wide[None, :], 0.0), axis=1)
        picked_place = jnp.sum(jnp.where(chosen, bal_place[None, :], 0.0), axis=1)
        row_sum, quality_sum, place_sum = lax.psum(
            (picked_rows, picked_quality, picked_place), ("dp", "grp")
        )
        row_now = row_sum[0].astype(jnp.bfloat16)
        quality_now = quality_sum[0]
        place_now = place_sum[0]
        dot_now = jnp.dot(relaid, row_now, preferred_element_type=jnp.float32)
        column_now = []
        for prior_step in range(turn_index):
            cross_term = (
                kept_quality[prior_step]
                * quality_now
                * jnp.dot(kept_rows[prior_step], row_now, preferred_element_type=jnp.float32)
                / feature_width
            )
            for earlier in range(prior_step):
                cross_term = cross_term - kept_columns[prior_step][earlier] * column_now[earlier]
            column_now.append(cross_term / kept_roots[prior_step])
        self_term = (
            quality_now
            * quality_now
            * jnp.dot(row_now, row_now, preferred_element_type=jnp.float32)
            / feature_width
            + RIDGE
        )
        for prior_step in range(turn_index):
            self_term = self_term - column_now[prior_step] * column_now[prior_step]
        root_now = jnp.sqrt(self_term)
        inner_sum = jnp.zeros_like(residual_gain)
        for prior_step in range(turn_index):
            inner_sum = inner_sum + chol_list[prior_step] * column_now[prior_step]
        ridge_hit = jnp.where(local_place == place_now, RIDGE, 0.0)
        new_entry = (
            bal_quality * quality_now * dot_now / feature_width + ridge_hit - inner_sum
        ) / root_now
        chol_list.append(new_entry)
        residual_gain = residual_gain - new_entry * new_entry
        kept_rows.append(row_now)
        kept_quality.append(quality_now)
        kept_columns.append(column_now)
        kept_roots.append(root_now)
    return (relaid, residual_gain, jnp.stack(chol_list))


def solution(mesh):
    return jax.shard_map(
        body,
        mesh=mesh,
        in_specs=(
            P(("dp", "grp"), None),
            P(("dp", "grp")),
            P(("dp", "grp")),
            P(),
            P(("dp", "grp")),
            P(("dp", "grp")),
            P(),
        ),
        out_specs=(P(("dp", "grp"), None), P(("dp", "grp")), P(None, ("dp", "grp"))),
        check_vma=False,
    )
```

profile of v0, /device:TPU:0, one launch (start us, length us, event | category | flops | bytes accessed | tf_op | source)
XLA Modules:
  0.0 117.8 jit_solution(18010897146661138979)
XLA Ops:
  0.6 1.4 %fusion.41 = (s32[1]{0:T(128)}, s32[1]{0:T(128)}, s32[1]{0:T(128)}, s32[1]{0:T(128)}) fusion(s32[4]{0:T(128)} %param.13), kind=kLoop, calls=%fused_computation.95 | loop fusion | bytes 32 | tf_op jit(solution)/shard_map/slice | solution.py:61
  5.2 1.0 fusion.1
  6.2 0.8 select_reduce_fusion
  6.9 0.7 add_add_fusion
  7.6 1.4 %fusion.38 = (f32[]{:T(128)}, f32[]{:T(128)}, f32[]{:T(128)}, f32[]{:T(128)}, bf16[256]{0:T(256)(128)(2,1)S(1)}) fusion(s32[]{:T(128)} %bitcast.13, s32[]{:T(128)} %bitcast.7, s32[]{:T(128)} %bitcast.10, s32[]{:T(128)} %bitcast.4, f32[256]{0:T(256)} %param.8, f32[256]{0:T(256)S(1)} %select_reduce_fusion, s32[]{:T(128)} %bitcast.50), kind=kLoop, calls=%fused_computation.81 | loop fusion | flops 4348 | bytes 2596 | tf_op jit(solution)/shard_map/reduce_sum | solution.py:66
  9.0 2.2 %scatter_custom_fusion.1 = bf16[512]{0:T(512)(128)(2,1)S(1)} fusion(s32[256]{0:T(256)S(1)} %get-tuple-element.45, bf16[256]{0:T(256)(128)(2,1)S(1)} %get-tuple-element.38, bf16[]{:T(256)} %constant.18.clone.1), kind=kCustom, calls=%fused_computation.93 | custom fusion | bytes 1026 | tf_op jit(solution)/shard_map/scatter | solution.py:36
  11.2 0.7 reshape.113
  11.9 8.3 %all-to-all-start.2 = ((bf16[16,2,16]{2,1,0:T(2,128)(2,1)}), bf16[16,2,16]{2,1,0:T(2,128)(2,1)S(1)}, u32[]{:S(2)}, u32[]{:S(2)}) async-start(bf16[16,2,16]{2,1,0:T(2,128)(2,1)} %reshape.113), calls=%async_computation.2 | async-start | bytes 16384 | tf_op jit(solution)/shard_map/all_to_all | solution.py:41
  20.2 3.1 %scatter_custom_fusion = bf16[512,1024]{1,0:T(8,128)(2,1)} fusion(s32[256]{0:T(256)S(1)} %get-tuple-element.45, bf16[256,1024]{1,0:T(8,128)(2,1)} %param.7, bf16[]{:T(256)} %constant.18.clone.1), kind=kCustom, calls=%fused_computation.6 | custom fusion | bytes 1049088 | tf_op jit(solution)/shard_map/scatter | solution.py:33
  23.3 4.1 %all-to-all-done.2 = bf16[16,2,16]{2,1,0:T(2,128)(2,1)S(1)} async-done(((bf16[16,2,16]{2,1,0:T(2,128)(2,1)}), bf16[16,2,16]{2,1,0:T(2,128)(2,1)S(1)}, u32[]{:S(2)}, u32[]{:S(2)}) %all-to-all-start.2) | async-done | bytes 1056 | tf_op jit(solution)/shard_map/all_to_all | solution.py:41
  27.4 0.1 reshape.204
  27.5 3.7 %all_to_all.20 = bf16[2,2,128]{2,1,0:T(2,128)(2,1)S(1)} all-to-all(bf16[2,2,128]{2,1,0:T(2,128)(2,1)S(1)} %reshape.204), channel_id=1, replica_groups=mesh['dp'=16,'grp'=2] {'grp'}, dimensions={0} | all-to-all | bytes 2048 | tf_op jit(solution)/shard_map/all_to_all | solution.py:44
  31.2 0.0 copy-start.1
  31.2 3.8 %all-to-all-start = ((bf16[16,2,16,1024]{3,2,1,0:T(8,128)(2,1)}), bf16[16,2,16,1024]{3,2,1,0:T(8,128)(2,1)S(1)}, u32[]{:S(2)}, u32[]{:S(2)}) async-start(bf16[16,2,16,1024]{3,2,1,0:T(8,128)(2,1)} %bitcast.1), calls=%async_computation | async-start | bytes 2097152 | tf_op jit(solution)/shard_map/all_to_all | solution.py:40
  35.1 0.7 select_reduce_fusion.1
  35.8 0.0 copy-done.1
  35.8 0.2 fusion.42
  36.0 0.2 fusion.43
  36.1 0.2 fusion.44
  36.3 0.2 fusion.45
  36.5 47.5 %all-reduce = (f32[]{:T(128)}, bf16[1,1024]{1,0:T(2,128)(2,1)S(1)}, bf16[1,1024]{1,0:T(2,128)(2,1)S(1)}, bf16[1,1024]{1,0:T(2,128)(2,1)S(1)}, bf16[1,1024]{1,0:T...) all-reduce(f32[]{:T(128)} %get-tuple-element.20, ...), channel_id=1, replica_groups=mesh['dp'=16,'grp'=2] {'dp','grp'}, use_global_device_ids=true, to_apply=%region_5.6 | all-reduce | flops 4104 | bytes 24640 | tf_op jit(solution)/shard_map/psum | solution.py:68
  91.9 0.7 fusion.17
  104.4 0.1 reshape.205
  104.5 0.0 all-to-all-done
  104.5 0.1 copy.27
  104.6 4.6 %all_to_all.21 = bf16[16,2,16,1024]{3,2,0,1:T(8,128)(2,1)S(1)} all-to-all(bf16[16,2,16,1024]{3,2,0,1:T(8,128)(2,1)S(1)} %copy.27), channel_id=1, replica_groups=mesh['dp'=16,'grp'=2] {'grp'}, dimensions={1} | all-to-all | bytes 2097152 | tf_op jit(solution)/shard_map/all_to_all | solution.py:43
  109.1 0.1 copy.28
  109.3 0.0 copy-start
  109.3 0.4 fusion.29
  109.6 0.4 fusion.27
  110.0 0.4 fusion.25
  110.4 0.0 copy-done
  110.4 0.4 fusion.23
  110.8 0.3 fusion
  111.1 2.6 %convert_multiply_fusion.4 = (f32[16,2,16]{2,0,1:T(8,128)S(1)}, f32[16,2,16]{2,0,1:T(8,128)S(1)}, f32[16,2,16]{2,0,1:T(8,128)S(1)}, f32[16,2,16]{2,0,1:T(8,128)S(1)}, f32[16,2,16]{2,0,1:T(8,128)S(1)}) fusion(f32[]{:T(128)} %get-tuple-element.21, f32[]{:T(128)} %get-tuple-element.27, f32[]{:T(128)} %get-tuple-element.29, f32[]{:T(128)} %get-tuple-element.31, ...), kind=kLoop, calls=%fused_computation.12 | loop fusion | flops 5632 | bytes 13328 | tf_op jit(solution)/shard_map/mul | solution.py:101
  113.7 0.1 mul.230
  113.8 0.1 mul.240
  113.9 0.1 mul.252
  114.0 0.1 mul.270
  114.1 0.1 reshape.125
  114.2 3.0 %multiply_subtract_fusion = (f32[512]{0:T(512)}, f32[512]{0:T(512)S(1)}, f32[512]{0:T(512)S(1)}, f32[512]{0:T(512)S(1)}, f32[512]{0:T(512)S(1)}) fusion(f32[512]{0:T(512)S(1)} %reshape.125, f32[]{:T(128)S(6)} %sqrt.15, f32[]{:T(128)S(6)} %div.115, f32[]{:T(128)S(6)} %div.113, f32[]{:T(128)S(6)} %div.111, f32[]{:T(128)} %get-tuple-element.32, s32[]{:T(128)S(6)} %mul.232, ...), kind=kLoop, calls=%fused_computation.64 | loop fusion | flops 23552 | bytes 28732 | tf_op jit(solution)/shard_map/sub | solution.py:104
  117.2 0.6 pad_maximum_fusion
  (17 shorter events, 0.2 us)
Async XLA Ops:
  11.9 15.6 %all-to-all-start.2 = ((bf16[16,2,16]{2,1,0:T(2,128)(2,1)}), bf16[16,2,16]{2,1,0:T(2,128)(2,1)S(1)}, u32[]{:S(2)}, u32[]{:S(2)}) async-start(bf16[16,2,16]{2,1,0:T(2,128)(2,1)} %reshape.113), calls=%async_computation.2 | async-start | bytes 16384 | tf_op jit(solution)/shard_map/all_to_all | solution.py:41
  31.2 4.6 %copy-start.1 = (bf16[256,1024]{1,0:T(8,128)(2,1)S(1)}, bf16[256,1024]{1,0:T(8,128)(2,1)}, u32[]{:S(2)}) copy-start(bf16[256,1024]{1,0:T(8,128)(2,1)} %param.7) | copy-start | bytes 1572868
  31.2 73.2 %all-to-all-start = ((bf16[16,2,16,1024]{3,2,1,0:T(8,128)(2,1)}), bf16[16,2,16,1024]{3,2,1,0:T(8,128)(2,1)S(1)}, u32[]{:S(2)}, u32[]{:S(2)}) async-start(bf16[16,2,16,1024]{3,2,1,0:T(8,128)(2,1)} %bitcast.1), calls=%async_computation | async-start | bytes 2097152 | tf_op jit(solution)/shard_map/all_to_all | solution.py:40
  109.3 1.2 copy-start
where the time goes:
time: 119 us; the launch traced here: 118 us
  blocking collectives  55.7 us (47%)
  between operations  23.6 us (20%)
  starting transfers between devices  12.1 us (10%)
  other arithmetic  10.7 us (9%)
  local copies, waits for them, and re-layouts  8.38 us (7%)
  waiting for transfers between devices  4.08 us (3%)
  matrix products  3.22 us (3%)
    psum x1, blocking collectives, body(): lax.psum((picked_rows, picked_quality, picked_place), ('dp', 'grp'))  47.5 us
    all_to_all x1, starting transfers between devices, body(): lax.all_to_all(send_quality, 'dp', split_axis=0, concat_axis=0, tiled=True)  8.34 us
    all_to_all x1, blocking collectives, body(): lax.all_to_all(first_hop[0], 'grp', split_axis=1, concat_axis=1, tiled=True)  4.58 us
    all_to_all x1, waiting for transfers between devices, body(): lax.all_to_all(send_quality, 'dp', split_axis=0, concat_axis=0, tiled=True)  4.08 us
    all_to_all x1, starting transfers between devices, body(): lax.all_to_all(send_rows, 'dp', split_axis=0, concat_axis=0, tiled=True)  3.79 us
    all_to_all x1, blocking collectives, body(): lax.all_to_all(first_hop[1], 'grp', split_axis=1, concat_axis=1, tiled=True)  3.69 us
    scatter x1, local copies, waits for them, and re-layouts, body(): jnp.zeros((balanced, feature_width), jnp.bfloat16).at[send_slot]  3.15 us
    sub x1, other arithmetic, body(): residual_gain = residual_gain - new_entry * new_entry  2.97 us
  transfers between devices with their start and end apart: 2, of which 1 were waited for; matrix products, arithmetic and copies ran while one was open for 5% of the time, Pallas kernels for 0%

commit v1 on v0

--- a/solution.py
+++ b/solution.py
@@ -66,7 +66,7 @@
         picked_quality = jnp.sum(jnp.where(chosen, quality_wide[None, :], 0.0), axis=1)
         picked_place = jnp.sum(jnp.where(chosen, bal_place[None, :], 0.0), axis=1)
         row_sum, quality_sum, place_sum = lax.psum(
-            (picked_rows, picked_quality, picked_place), ("dp", "grp")
+            lax.psum((picked_rows, picked_quality, picked_place), "grp"), "dp"
         )
         row_now = row_sum[0].astype(jnp.bfloat16)
         quality_now = quality_sum[0]

time: 119 us -> 158 us (1.33)
  blocking collectives: 55.7 us -> 95.3 us
    psum x1 -> x2, blocking collectives: 47.5 us -> 87.1 us  [the longest x1 82.4 us: body(): lax.psum(lax.psum((picked_rows, picked_quality, picked_place), 'grp'), 'dp')]
  transfers between devices with their start and end apart: 2 -> 2, of which waited for: 1 -> 1; matrix products, arithmetic and copies ran while one was open for 5% -> 3% of each run, Pallas kernels for 0% -> 0%
where the time goes in v1:
time: 158 us; the launch traced here: 157 us
  blocking collectives  95.3 us (60%)
  between operations  23.6 us (15%)
  starting transfers between devices  12.1 us (8%)
  other arithmetic  10.7 us (7%)
  local copies, waits for them, and re-layouts  8.38 us (5%)
  waiting for transfers between devices  4.08 us (3%)
  matrix products  3.22 us (2%)
    psum x1, blocking collectives, body(): lax.psum(lax.psum((picked_rows, picked_quality, picked_place), 'grp'), 'dp')  82.4 us
    all_to_all x1, starting transfers between devices, body(): lax.all_to_all(send_quality, 'dp', split_axis=0, concat_axis=0, tiled=True)  8.34 us
    psum x1, blocking collectives, body(): lax.psum((picked_rows, picked_quality, picked_place), 'grp')  4.64 us
    all_to_all x1, blocking collectives, body(): lax.all_to_all(first_hop[0], 'grp', split_axis=1, concat_axis=1, tiled=True)  4.58 us
    all_to_all x1, waiting for transfers between devices, body(): lax.all_to_all(send_quality, 'dp', split_axis=0, concat_axis=0, tiled=True)  4.08 us
    all_to_all x1, starting transfers between devices, body(): lax.all_to_all(send_rows, 'dp', split_axis=0, concat_axis=0, tiled=True)  3.79 us
    all_to_all x1, blocking collectives, body(): lax.all_to_all(first_hop[1], 'grp', split_axis=1, concat_axis=1, tiled=True)  3.69 us
  transfers between devices with their start and end apart: 2, of which 1 were waited for; matrix products, arithmetic and copies ran while one was open for 3% of the time, Pallas kernels for 0%

profile of v1, /device:TPU:0, one launch (start us, length us, event | category | flops | bytes accessed | tf_op | source)
XLA Modules:
  0.0 157.4 jit_solution(10076983927141514107)
XLA Ops:
  0.6 1.4 fusion.41
  5.2 1.0 fusion.1
  6.2 0.8 select_reduce_fusion
  6.9 0.7 add_add_fusion
  7.6 1.4 fusion.38
  9.0 2.2 %scatter_custom_fusion.1 = bf16[512]{0:T(512)(128)(2,1)S(1)} fusion(s32[256]{0:T(256)S(1)} %get-tuple-element.57, bf16[256]{0:T(256)(128)(2,1)S(1)} %get-tuple-element.50, bf16[]{:T(256)} %constant.18.clone.1), kind=kCustom, calls=%fused_computation.93 | custom fusion | bytes 1026 | tf_op jit(solution)/shard_map/scatter | solution.py:36
  11.2 0.7 reshape.113
  11.8 8.3 %all-to-all-start.2 = ((bf16[16,2,16]{2,1,0:T(2,128)(2,1)}), bf16[16,2,16]{2,1,0:T(2,128)(2,1)S(1)}, u32[]{:S(2)}, u32[]{:S(2)}) async-start(bf16[16,2,16]{2,1,0:T(2,128)(2,1)} %reshape.113), calls=%async_computation.2 | async-start | bytes 16384 | tf_op jit(solution)/shard_map/all_to_all | solution.py:41
  20.2 3.1 %scatter_custom_fusion = bf16[512,1024]{1,0:T(8,128)(2,1)} fusion(s32[256]{0:T(256)S(1)} %get-tuple-element.57, bf16[256,1024]{1,0:T(8,128)(2,1)} %param.7, bf16[]{:T(256)} %constant.18.clone.1), kind=kCustom, calls=%fused_computation.6 | custom fusion | bytes 1049088 | tf_op jit(solution)/shard_map/scatter | solution.py:33
  23.3 4.1 %all-to-all-done.2 = bf16[16,2,16]{2,1,0:T(2,128)(2,1)S(1)} async-done(((bf16[16,2,16]{2,1,0:T(2,128)(2,1)}), bf16[16,2,16]{2,1,0:T(2,128)(2,1)S(1)}, u32[]{:S(2)}, u32[]{:S(2)}) %all-to-all-start.2) | async-done | bytes 1056 | tf_op jit(solution)/shard_map/all_to_all | solution.py:41
  27.4 0.1 reshape.196
  27.5 3.7 %all_to_all.20 = bf16[2,2,128]{2,1,0:T(2,128)(2,1)S(1)} all-to-all(bf16[2,2,128]{2,1,0:T(2,128)(2,1)S(1)} %reshape.196), channel_id=1, replica_groups=mesh['dp'=16,'grp'=2] {'grp'}, dimensions={0} | all-to-all | bytes 2048 | tf_op jit(solution)/shard_map/all_to_all | solution.py:44
  31.2 0.0 copy-start.1
  31.2 3.8 %all-to-all-start = ((bf16[16,2,16,1024]{3,2,1,0:T(8,128)(2,1)}), bf16[16,2,16,1024]{3,2,1,0:T(8,128)(2,1)S(1)}, u32[]{:S(2)}, u32[]{:S(2)}) async-start(bf16[16,2,16,1024]{3,2,1,0:T(8,128)(2,1)} %bitcast.1), calls=%async_computation | async-start | bytes 2097152 | tf_op jit(solution)/shard_map/all_to_all | solution.py:40
  35.1 0.6 select_reduce_fusion.1
  35.7 0.0 copy-done.1
  35.7 0.2 fusion.42
  35.9 0.2 fusion.43
  36.1 0.2 fusion.44
  36.3 0.2 fusion.45
  36.5 4.6 %all-reduce.1 = (f32[1]{0:T(128)}, f32[1,1024]{1,0:T(1,128)S(1)}, f32[1,1024]{1,0:T(1,128)S(1)}, f32[1,1024]{1,0:T(1,128)S(1)}, f32[1,1024]{1,0:T(1,128)S(1)}, /...) all-reduce(f32[1]{0:T(128)} %bitcast.5, ...), channel_id=1, replica_groups=mesh['dp'=16,'grp'=2] {'grp'}, use_global_device_ids=true, to_apply=%region_5.6 | all-reduce | flops 4104 | bytes 32832 | tf_op jit(solution)/shard_map/psum | solution.py:69
  41.1 82.4 %all-reduce = (f32[]{:T(128)}, bf16[1,1024]{1,0:T(2,128)(2,1)S(1)}, bf16[1,1024]{1,0:T(2,128)(2,1)S(1)}, bf16[1,1024]{1,0:T(2,128)(2,1)S(1)}, bf16[1,1024]{1,0:T...) all-reduce(f32[]{:T(128)} %bitcast.6, ...), channel_id=1, replica_groups=mesh['dp'=16,'grp'=2] {'dp'}, use_global_device_ids=true, to_apply=%region_6.7 | all-reduce | flops 4104 | bytes 24640 | tf_op jit(solution)/shard_map/psum | solution.py:68
  131.5 0.7 fusion.17
  143.9 0.1 reshape.197
  144.0 0.0 all-to-all-done
  144.0 0.1 copy.27
  144.1 4.6 %all_to_all.21 = bf16[16,2,16,1024]{3,2,0,1:T(8,128)(2,1)S(1)} all-to-all(bf16[16,2,16,1024]{3,2,0,1:T(8,128)(2,1)S(1)} %copy.27), channel_id=1, replica_groups=mesh['dp'=16,'grp'=2] {'grp'}, dimensions={1} | all-to-all | bytes 2097152 | tf_op jit(solution)/shard_map/all_to_all | solution.py:43
  148.7 0.1 copy.28
  148.8 0.0 copy-start
  148.8 0.4 fusion.29
  149.2 0.4 fusion.27
  149.6 0.4 fusion.25
  150.0 0.0 copy-done
  150.0 0.4 fusion.23
  150.4 0.3 fusion
  150.6 2.6 %convert_multiply_fusion.4 = (f32[16,2,16]{2,0,1:T(8,128)S(1)}, f32[16,2,16]{2,0,1:T(8,128)S(1)}, f32[16,2,16]{2,0,1:T(8,128)S(1)}, f32[16,2,16]{2,0,1:T(8,128)S(1)}, f32[16,2,16]{2,0,1:T(8,128)S(1)}) fusion(f32[]{:T(128)} %get-tuple-element.21, f32[]{:T(128)} %get-tuple-element.27, f32[]{:T(128)} %get-tuple-element.29, f32[]{:T(128)} %get-tuple-element.31, ...), kind=kLoop, calls=%fused_computation.12 | loop fusion | flops 5632 | bytes 13328 | tf_op jit(solution)/shard_map/mul | solution.py:101
  153.3 0.1 mul.230
  153.4 0.1 mul.240
  153.5 0.1 mul.252
  153.6 0.1 mul.270
  153.7 0.1 reshape.117
  153.8 3.0 %multiply_subtract_fusion = (f32[512]{0:T(512)}, f32[512]{0:T(512)S(1)}, f32[512]{0:T(512)S(1)}, f32[512]{0:T(512)S(1)}, f32[512]{0:T(512)S(1)}) fusion(f32[512]{0:T(512)S(1)} %reshape.117, f32[]{:T(128)S(6)} %sqrt.15, f32[]{:T(128)S(6)} %div.115, f32[]{:T(128)S(6)} %div.113, f32[]{:T(128)S(6)} %div.111, f32[]{:T(128)} %get-tuple-element.32, s32[]{:T(128)S(6)} %mul.232, ...), kind=kLoop, calls=%fused_computation.64 | loop fusion | flops 23552 | bytes 28732 | tf_op jit(solution)/shard_map/sub | solution.py:104
  156.7 0.6 pad_maximum_fusion
  (17 shorter events, 0.2 us)
Async XLA Ops:
  11.8 15.6 %all-to-all-start.2 = ((bf16[16,2,16]{2,1,0:T(2,128)(2,1)}), bf16[16,2,16]{2,1,0:T(2,128)(2,1)S(1)}, u32[]{:S(2)}, u32[]{:S(2)}) async-start(bf16[16,2,16]{2,1,0:T(2,128)(2,1)} %reshape.113), calls=%async_computation.2 | async-start | bytes 16384 | tf_op jit(solution)/shard_map/all_to_all | solution.py:41
  31.2 4.5 %copy-start.1 = (bf16[256,1024]{1,0:T(8,128)(2,1)S(1)}, bf16[256,1024]{1,0:T(8,128)(2,1)}, u32[]{:S(2)}) copy-start(bf16[256,1024]{1,0:T(8,128)(2,1)} %param.7) | copy-start | bytes 1572868
  31.2 112.8 %all-to-all-start = ((bf16[16,2,16,1024]{3,2,1,0:T(8,128)(2,1)}), bf16[16,2,16,1024]{3,2,1,0:T(8,128)(2,1)S(1)}, u32[]{:S(2)}, u32[]{:S(2)}) async-start(bf16[16,2,16,1024]{3,2,1,0:T(8,128)(2,1)} %bitcast.1), calls=%async_computation | async-start | bytes 2097152 | tf_op jit(solution)/shard_map/all_to_all | solution.py:40
  148.8 1.2 copy-start
